TPU v7x, 128 devices: a whole 4x4x4 slice. The times are simulated.
128 devices in a mesh: row: 8 (over x_hi, z), rep: 16 (over x_lo, y, core).
Axes of the slice: x: 4 (x_hi: 2, x_lo: 2; x = x_hi * 2 + x_lo), y: 4, z: 4, core: 2. Of those that a mesh axis runs over, the one named last changes fastest.
Arguments:
- features: bfloat16 [32768, 256], P('row'), may hold values from 0 to 2
- self_weight: bfloat16 [256, 256], replicated, may hold values from -0.375 to 0.375
- neigh_weight: bfloat16 [256, 256], replicated, may hold values from -0.375 to 0.375
- out_bias: float32 [256], replicated, may hold values from -4 to 4
- tile_masks: int32 [32768, 128, 128], P('row', 'rep'), may hold values 0 or 1
- tile_live: int32 [256, 128], P('row', 'rep'), may hold values from 0 to 1, as said below
- tile_columns: int32 [256, 128], P('row', 'rep'), may hold values from 0 to 1
- node_degree: int32 [32768], P(('row', 'rep')), may hold values from 128 to 511
- cotangent: bfloat16 [32768, 256], P(('row', 'rep')), may hold values from -6 to 6
Outputs:
- hidden_out: bfloat16 [32768, 256], P(('row', 'rep'))
- grad_features: bfloat16 [32768, 256], P(('row', 'rep'))
- grad_self: float32 [256, 256], replicated
- grad_neigh: float32 [256, 256], replicated
- grad_bias: float32 [256], replicated
Inputs may be any that keep to these rules, and one draw needn't show every extreme that they name: `tile_masks`: an edge bit; bits of slots without a tile are not read. `tile_live`: 1 where the slot holds a tile. `tile_columns`: the covered block among the 2 blocks of that column set and panel.
All inputs are finite; a program needn't handle non-finite values. No bound on the sum of `tile_masks` on one device may be relied on, other than what follows from the above.
Results may differ from a plain program's by a relative error of at most 0.0053.
Values may be sent and summed in bfloat16 or wider, within the bound.
A program may use at most 128 MiB of HBM per device.

v0:
```python
import math
import jax
import jax.numpy as jnp
from jax import lax
from jax.sharding import PartitionSpec as P


def activation(values):
    return jax.nn.gelu(values, approximate=True)


def per_device(
    features,
    self_weight,
    neigh_weight,
    out_bias,
    tile_masks,
    tile_live,
    tile_columns,
    node_degree,
    cotangent,
):
    row_devices = lax.axis_size("row")
    rep_devices = lax.axis_size("rep")
    panel_rows, width = features.shape
    share_rows = node_degree.shape[0]
    panel_count = tile_masks.shape[1]
    tile_size = tile_masks.shape[2]
    block_rows = panel_rows // tile_size
    set_blocks = share_rows // tile_size
    column_rows = panel_count * share_rows
    contract_first = (((0,), (0,)), ((), ()))
    contract_second = (((1,), (1,)), ((), ()))
    block_ids = jnp.arange(set_blocks, dtype=jnp.int32)
    selected = (tile_columns[:, :, None] == block_ids[None, None, :]) & (tile_live[:, :, None] != 0)
    keeper = selected.astype(jnp.bfloat16)
    dense = tile_masks.reshape(block_rows, tile_size, panel_count, 1, tile_size).astype(
        jnp.bfloat16
    )
    dense = (dense * keeper[:, None, :, :, None]).reshape(panel_rows, column_rows)
    own = lax.dynamic_slice_in_dim(features, lax.axis_index("rep") * share_rows, share_rows, 0)
    strip = dense
    partial_sums = jnp.dot(
        strip, lax.all_gather(own, "row", axis=0, tiled=True), preferred_element_type=jnp.float32
    )
    agg_sum = lax.psum_scatter(partial_sums, "rep", scatter_dimension=0, tiled=True)
    degree = node_degree.astype(jnp.float32)[:, None]
    mean = (agg_sum / degree).astype(jnp.bfloat16)
    pre = (
        jnp.dot(own, self_weight, preferred_element_type=jnp.float32)
        + jnp.dot(mean, neigh_weight, preferred_element_type=jnp.float32)
        + out_bias
    )
    result, pull = jax.vjp(activation, pre)
    hidden_out = result.astype(jnp.bfloat16)
    dpre = pull(cotangent.astype(jnp.float32))[0]
    dpre_b = dpre.astype(jnp.bfloat16)
    scale = 1.0 / math.sqrt(share_rows * row_devices * rep_devices)
    self_term = (
        lax.dot_general(own, dpre_b, contract_first, preferred_element_type=jnp.float32) * scale
    )
    neigh_term = (
        lax.dot_general(mean, dpre_b, contract_first, preferred_element_type=jnp.float32) * scale
    )
    bias_term = jnp.sum(dpre, axis=0) * scale
    grad_self, grad_neigh, grad_bias = lax.psum((self_term, neigh_term, bias_term), ("row", "rep"))
    message = (
        lax.dot_general(dpre_b, neigh_weight, contract_second, preferred_element_type=jnp.float32)
        / degree
    ).astype(jnp.bfloat16)
    direct = lax.dot_general(
        dpre_b, self_weight, contract_second, preferred_element_type=jnp.float32
    )
    strip = dense
    partial_back = lax.dot_general(
        strip,
        lax.all_gather(message, "rep", axis=0, tiled=True),
        contract_first,
        preferred_element_type=jnp.float32,
    )
    spread = lax.psum_scatter(
        partial_back.astype(jnp.bfloat16), "row", scatter_dimension=0, tiled=True
    ).astype(jnp.float32)
    grad_features = (direct + spread).astype(jnp.bfloat16)
    return (hidden_out, grad_features, grad_self, grad_neigh, grad_bias)


def solution(mesh):
    return jax.shard_map(
        per_device,
        mesh=mesh,
        in_specs=(
            P("row", None),
            P(),
            P(),
            P(),
            P("row", "rep", None),
            P("row", "rep"),
            P("row", "rep"),
            P(("row", "rep")),
            P(("row", "rep"), None),
        ),
        out_specs=(P(("row", "rep"), None), P(("row", "rep"), None), P(), P(), P()),
        check_vma=False,
    )
```

profile of v0, /device:TPU:1, one launch (start us, length us, event | category | flops | bytes accessed | tf_op | source)
XLA Modules:
  0.0 428.5 jit_solution(4350122207436884132)
XLA Ops:
  7.2 0.0 all-gather.3.cloned.1.call-start
  7.2 1.5 copy-done
  8.8 0.7 constant_dynamic-slice_fusion
  9.5 0.0 reduce-scatter.3.cloned.1.call-start
  9.5 0.8 copy.14
  10.3 0.7 broadcast_compare_fusion
  11.0 0.1 copy.15
  11.1 6.3 %convert_element_type.45 = bf16[4096,8,128]{2,1,0:T(8,128)(2,1)S(1)} convert(s32[4096,8,128]{2,1,0:T(8,128)} %param.13) | non-fusion elementwise | flops 4194304 | bytes 25165824 | tf_op jit(solution)/shard_map/convert_element_type | solution.py:37
  17.4 0.1 fusion.13
  17.5 19.8 %broadcast_multiply_fusion = bf16[32,128,8,2,128]{4,3,2,1,0:T(2,128)(2,1)} fusion(bf16[32,8,2]{2,1,0:T(8,128)(2,1)S(1)} %fusion.13, bf16[32,128,8,128]{3,2,1,0:T(8,128)(2,1)S(1)} %bitcast.15), kind=kLoop, calls=%fused_computation | loop fusion | flops 8388608 | bytes 25166848 | tf_op jit(solution)/shard_map/mul | solution.py:40
  37.3 27.8 %mul.80 = bf16[4096,2048]{1,0:T(8,128)(2,1)} reshape(bf16[32,128,8,2,128]{4,3,2,1,0:T(2,128)(2,1)} %broadcast_multiply_fusion) | data formatting | bytes 33554432 | tf_op jit(solution)/shard_map/mul | solution.py:40
  65.1 0.0 all-gather.3.cloned.1.call-done
  65.2 12.6 %fusion.17 = f32[4096,256]{1,0:T(8,128)} fusion(bf16[4096,2048]{1,0:T(8,128)(2,1)} %mul.80, bf16[2048,256]{1,0:T(8,128)(2,1)} %all-gather.3.cloned.1.call-done), kind=kOutput, calls=%fused_computation.33 | convolution fusion | flops 4294967296 | bytes 22020096 | tf_op jit(solution)/shard_map/dot_general | solution.py:43
  77.8 0.0 reduce-scatter.3.cloned.1.call-update
  77.8 0.0 all-gather.5.cloned.1.call-start
  77.9 0.2 fusion.16
  78.1 66.0 %reduce-scatter.3.cloned.1.call-done = f32[256,256]{1,0:T(8,128)} async-done(((f32[4096,256]{1,0:T(8,128)}), f32[256,256]{1,0:T(8,128)}) %reduce-scatter.3.cloned.1.call-update) | async-done | bytes 262160 | tf_op jit(solution)/shard_map/reduce_scatter | solution.py:46
  144.1 2.0 fusion.14
  146.1 0.9 fusion.2
  147.0 0.0 all-gather.5.cloned.1.call-update
  147.0 0.2 reduce-scatter.5.cloned.1.call-start
  147.3 36.9 %all-gather.5.cloned.1.call-done = bf16[4096,256]{1,0:T(8,128)(2,1)} async-done(((bf16[256,256]{1,0:T(8,128)(2,1)}), bf16[4096,256]{1,0:T(8,128)(2,1)}) %all-gather.5.cloned.1.call-update) | async-done | bytes 2097168 | tf_op jit(solution)/shard_map/all_gather | solution.py:77
  184.1 12.3 %convolution_convert_fusion = bf16[2048,256]{1,0:T(8,128)(2,1)} fusion(bf16[4096,2048]{1,0:T(8,128)(2,1)} %mul.80, bf16[4096,256]{1,0:T(8,128)(2,1)} %all-gather.5.cloned.1.call-done), kind=kOutput, calls=%fused_computation.1 | convolution fusion | flops 4295491584 | bytes 19922944 | tf_op jit(solution)/shard_map/dot_general | solution.py:75
  196.4 0.0 all-reduce.3.cloned.1.call-start
  196.5 0.9 convolution_multiply_fusion.1
  197.4 1.0 convolution_multiply_fusion
  198.5 66.0 %psum.23 = f32[256]{0:T(256)} all-reduce(f32[256]{0:T(256)S(1)} %broadcast_multiply_fusion.1), channel_id=1, replica_groups=mesh['row'=8,'rep'=16] {'row','rep'}, use_global_device_ids=true, to_apply=%region_5.0 | all-reduce | flops 256 | bytes 2048 | tf_op jit(solution)/shard_map/psum | solution.py:66
  264.4 1.8 reduce-scatter.5.cloned.1.call-done
  266.2 1.8 fusion.1
  268.0 150.7 %all-reduce.3.cloned.1.call-done = (f32[256,256]{1,0:T(8,128)}, f32[256,256]{1,0:T(8,128)}) async-done(((f32[256,256]{1,0:T(8,128)}, f32[256,256]{1,0:T(8,128)}), (f32[256,256]{1,0:T(8,128)}, f32[256,256]{1,0:T(8,128)})) %all-reduce.3.cloned.1.call-update) | async-done | bytes 524304 | tf_op jit(solution)/shard_map/psum | solution.py:66
  418.6 1.7 copy.18
  420.3 1.7 copy.19
  (22 shorter events, 0.1 us)
Async XLA Ops:
  7.2 1.6 copy-start
  7.2 58.0 %all-gather.3.cloned.1.call-start = ((), (), s32[]{:S(2)}) async-start(), calls=%async_computation.2 | async-start | bytes 1179648 | tf_op jit(solution)/shard_map/all_gather | solution.py:44
  9.5 134.6 %reduce-scatter.3.cloned.1.call-start = ((), (), s32[]{:S(2)}) async-start(), calls=%async_computation.3 | async-start | bytes 4456448 | tf_op jit(solution)/shard_map/reduce_scatter | solution.py:46
  65.1 12.7 %copy-start.4 = (s32[256]{0:T(256)S(1)}, s32[256]{0:T(256)}, u32[]{:S(2)}) copy-start(s32[256]{0:T(256)} %param.16) | copy-start | bytes 3076
  65.1 12.8 %copy-start.2 = (bf16[256,256]{1,0:T(8,128)(2,1)S(1)}, bf16[256,256]{1,0:T(8,128)(2,1)}, u32[]{:S(2)}) copy-start(bf16[256,256]{1,0:T(8,128)(2,1)} %constant_dynamic-slice_fusion) | copy-start | bytes 393220
  65.1 12.8 %copy-start.3 = (bf16[256,256]{1,0:T(8,128)(2,1)S(1)}, bf16[256,256]{1,0:T(8,128)(2,1)}, u32[]{:S(2)}) copy-start(bf16[256,256]{1,0:T(8,128)(2,1)} %param.10) | copy-start | bytes 393220
  65.1 79.0 %copy-start.6 = (bf16[256,256]{1,0:T(8,128)(2,1)S(1)}, bf16[256,256]{1,0:T(8,128)(2,1)}, u32[]{:S(2)}) copy-start(bf16[256,256]{1,0:T(8,128)(2,1)} %param.17) | copy-start | bytes 393220
  65.1 78.9 %copy-start.7 = (bf16[256,256]{1,0:T(8,128)(2,1)S(1)}, bf16[256,256]{1,0:T(8,128)(2,1)}, u32[]{:S(2)}) copy-start(bf16[256,256]{1,0:T(8,128)(2,1)} %param.11) | copy-start | bytes 393220
  65.1 78.9 %copy-start.8 = (f32[256]{0:T(256)S(1)}, f32[256]{0:T(256)}, u32[]{:S(2)}) copy-start(f32[256]{0:T(256)} %param.12) | copy-start | bytes 3076
  77.8 106.3 %all-gather.5.cloned.1.call-start = ((), (), s32[]{:S(2)}) async-start(), calls=%async_computation.4 | async-start | bytes 2228224 | tf_op jit(solution)/shard_map/all_gather | solution.py:77
  147.0 50.4 %copy-start.5 = (f32[256,256]{1,0:T(8,128)S(1)}, f32[256,256]{1,0:T(8,128)}, u32[]{:S(2)}) copy-start(f32[256,256]{1,0:T(8,128)} %reduce-scatter.3.cloned.1.call-done) | copy-start | bytes 786436
  147.0 274.9 %copy-start.1 = (bf16[4096,256]{1,0:T(8,128)(2,1)S(1)}, bf16[4096,256]{1,0:T(8,128)(2,1)}, u32[]{:S(2)}) copy-start(bf16[4096,256]{1,0:T(8,128)(2,1)} %param.9) | copy-start | bytes 6291460
  147.0 119.2 %reduce-scatter.5.cloned.1.call-start = ((), (), s32[]{:S(2)}) async-start(), calls=%async_computation.5 | async-start | bytes 1179648 | tf_op jit(solution)/shard_map/reduce_scatter | solution.py:81
  196.4 222.2 %all-reduce.3.cloned.1.call-start = ((), (), s32[]{:S(2)}) async-start(), calls=%async_computation.6 | async-start | bytes 1048576 | tf_op jit(solution)/shard_map/psum | solution.py:66
Sparse Core Ops, SparseCore 0:
  11.0 48.4 all-gather.2
  77.9 66.0 reduce-scatter.2
  147.1 36.9 all-gather.4
  196.6 69.5 reduce-scatter.4
  272.3 146.2 all-reduce.2
where the time goes:
time: 430 us; the launch traced here: 429 us
  waiting for transfers between devices  255 us (59%)
  blocking collectives  66 us (15%)
  local copies, waits for them, and re-layouts  34.2 us (8%)
  matrix products  31.7 us (7%)
  other arithmetic  27 us (6%)
  between operations  13.9 us (3%)
    psum x1, waiting for transfers between devices, per_device(): lax.psum((self_term, neigh_term, bias_term), ('row', 'rep'))  151 us
    reduce_scatter x1, waiting for transfers between devices, per_device(): lax.psum_scatter(partial_sums, 'rep', scatter_dimension=0, tiled=True)  66 us
    psum x1, blocking collectives, per_device(): lax.psum((self_term, neigh_term, bias_term), ('row', 'rep'))  66 us
    all_gather x1, waiting for transfers between devices, per_device(): lax.all_gather(message, 'rep', axis=0, tiled=True)  36.9 us
    mul x1, local copies, waits for them, and re-layouts, per_device(): dense * keeper[:, None, :, :, None]  27.8 us
    mul x1, other arithmetic, per_device(): dense * keeper[:, None, :, :, None]  19.8 us
    dot_general x1, matrix products, per_device(): jnp.dot(strip, lax.all_gather(own, 'row', axis=0, tiled=True), preferred_...  12.6 us
    dot_general x1, matrix products, per_device(): lax.dot_general(strip, lax.all_gather(message, 'rep', axis=0, tiled=True)...  12.3 us
  transfers between devices with their start and end apart: 5, of which 4 were waited for; matrix products, arithmetic and copies ran while one was open for 14% of the time, Pallas kernels for 0%

commit v1 on v0

--- a/solution.py
+++ b/solution.py
@@ -3,6 +3,11 @@
 import jax.numpy as jnp
 from jax import lax
 from jax.sharding import PartitionSpec as P
+
+
+def axis_by_axis(x, one, other):
+    half = lax.psum(x, one)
+    return lax.psum(half, other)
 
 
 def activation(values):
@@ -63,7 +68,9 @@
         lax.dot_general(mean, dpre_b, contract_first, preferred_element_type=jnp.float32) * scale
     )
     bias_term = jnp.sum(dpre, axis=0) * scale
-    grad_self, grad_neigh, grad_bias = lax.psum((self_term, neigh_term, bias_term), ("row", "rep"))
+    grad_self, grad_neigh, grad_bias = axis_by_axis(
+        (self_term, neigh_term, bias_term), "rep", "row"
+    )
     message = (
         lax.dot_general(dpre_b, neigh_weight, contract_second, preferred_element_type=jnp.float32)
         / degree

time: 430 us -> 479 us (1.11)
  waiting for transfers between devices: 255 us -> 317 us
  blocking collectives: 66 us -> 48.1 us
    psum x1 -> x2, waiting for transfers between devices: 151 us -> 190 us  [the longest x1 108 us: axis_by_axis(): half = lax.psum(x, one)]
    reduce_scatter x1, waiting for transfers between devices: 1.76 us -> 26.9 us  [per_device(): lax.psum_scatter(partial_back.astype(jnp.bfloat16), 'row', scatter_dimens...]
    psum x1 -> x2, blocking collectives: 66 us -> 48.1 us  [the longest x1 27.3 us: axis_by_axis(): half = lax.psum(x, one)]
  transfers between devices with their start and end apart: 5 -> 6, of which waited for: 4 -> 5; matrix products, arithmetic and copies ran while one was open for 14% -> 15% of each run, Pallas kernels for 0% -> 0%
where the time goes in v1:
time: 479 us; the launch traced here: 473 us
  waiting for transfers between devices  317 us (66%)
  blocking collectives  48.1 us (10%)
  local copies, waits for them, and re-layouts  34.2 us (7%)
  matrix products  32.7 us (7%)
  other arithmetic  27 us (6%)
  between operations  14.2 us (3%)
    psum x1, waiting for transfers between devices, axis_by_axis(): half = lax.psum(x, one)  108 us
    psum x1, waiting for transfers between devices, axis_by_axis(): return lax.psum(half, other)  81.9 us
    reduce_scatter x1, waiting for transfers between devices, per_device(): lax.psum_scatter(partial_sums, 'rep', scatter_dimension=0, tiled=True)  66 us
    all_gather x1, waiting for transfers between devices, per_device(): lax.all_gather(message, 'rep', axis=0, tiled=True)  33.9 us
    mul x1, local copies, waits for them, and re-layouts, per_device(): dense * keeper[:, None, :, :, None]  27.7 us
    psum x1, blocking collectives, axis_by_axis(): half = lax.psum(x, one)  27.3 us
    reduce_scatter x1, waiting for transfers between devices, per_device(): lax.psum_scatter(partial_back.astype(jnp.bfloat16), 'row', scatter_dimens...  26.9 us
    psum x1, blocking collectives, axis_by_axis(): return lax.psum(half, other)  20.8 us
  transfers between devices with their start and end apart: 6, of which 5 were waited for; matrix products, arithmetic and copies ran while one was open for 15% of the time, Pallas kernels for 0%

profile of v1, /device:TPU:1, one launch (start us, length us, event | category | flops | bytes accessed | tf_op | source)
XLA Modules:
  0.0 473.2 jit_solution(12892991152929946545)
XLA Ops:
  7.2 0.0 all-gather.3.cloned.1.call-start
  7.2 1.5 copy-done
  8.8 0.7 constant_dynamic-slice_fusion
  9.5 0.0 reduce-scatter.3.cloned.1.call-start
  9.5 0.8 copy.14
  10.3 0.7 broadcast_compare_fusion
  11.0 0.1 copy.15
  11.1 6.3 %convert_element_type.45 = bf16[4096,8,128]{2,1,0:T(8,128)(2,1)S(1)} convert(s32[4096,8,128]{2,1,0:T(8,128)} %param.13) | non-fusion elementwise | flops 4194304 | bytes 25165824 | tf_op jit(solution)/shard_map/convert_element_type | solution.py:42
  17.4 0.1 fusion.13
  17.5 19.8 %broadcast_multiply_fusion = bf16[32,128,8,2,128]{4,3,2,1,0:T(2,128)(2,1)} fusion(bf16[32,8,2]{2,1,0:T(8,128)(2,1)S(1)} %fusion.13, bf16[32,128,8,128]{3,2,1,0:T(8,128)(2,1)S(1)} %bitcast.15), kind=kLoop, calls=%fused_computation | loop fusion | flops 8388608 | bytes 25166848 | tf_op jit(solution)/shard_map/mul | solution.py:45
  37.3 27.7 %mul.80 = bf16[4096,2048]{1,0:T(8,128)(2,1)} reshape(bf16[32,128,8,2,128]{4,3,2,1,0:T(2,128)(2,1)} %broadcast_multiply_fusion) | data formatting | bytes 33554432 | tf_op jit(solution)/shard_map/mul | solution.py:45
  65.1 12.6 %fusion.17 = f32[4096,256]{1,0:T(8,128)} fusion(bf16[4096,2048]{1,0:T(8,128)(2,1)} %mul.80, bf16[2048,256]{1,0:T(8,128)(2,1)} %all-gather.3.cloned.1.call-done), kind=kOutput, calls=%fused_computation.33 | convolution fusion | flops 4294967296 | bytes 22020096 | tf_op jit(solution)/shard_map/dot_general | solution.py:48
  77.8 0.0 all-gather.5.cloned.1.call-start
  77.9 0.2 fusion.16
  78.1 66.0 %reduce-scatter.3.cloned.1.call-done = f32[256,256]{1,0:T(8,128)} async-done(((f32[4096,256]{1,0:T(8,128)}), f32[256,256]{1,0:T(8,128)}) %reduce-scatter.3.cloned.1.call-update) | async-done | bytes 262160 | tf_op jit(solution)/shard_map/reduce_scatter | solution.py:51
  144.1 2.0 fusion.14
  146.1 0.9 fusion.2
  147.0 0.0 all-reduce.5.cloned.1.call-start
  147.1 0.9 convolution_multiply_fusion.1
  148.0 2.0 convolution_multiply_fusion
  150.0 0.2 reduce-scatter.5.cloned.1.call-start
  150.2 33.9 %all-gather.5.cloned.1.call-done = bf16[4096,256]{1,0:T(8,128)(2,1)} async-done(((bf16[256,256]{1,0:T(8,128)(2,1)}), bf16[4096,256]{1,0:T(8,128)(2,1)}) %all-gather.5.cloned.1.call-update) | async-done | bytes 2097168 | tf_op jit(solution)/shard_map/all_gather | solution.py:84
  184.1 12.3 %convolution_convert_fusion = bf16[2048,256]{1,0:T(8,128)(2,1)} fusion(bf16[4096,2048]{1,0:T(8,128)(2,1)} %mul.80, bf16[4096,256]{1,0:T(8,128)(2,1)} %all-gather.5.cloned.1.call-done), kind=kOutput, calls=%fused_computation.1 | convolution fusion | flops 4295491584 | bytes 19922944 | tf_op jit(solution)/shard_map/dot_general | solution.py:82
  196.4 0.0 all-reduce.7.cloned.1.call-start
  196.5 107.9 %all-reduce.5.cloned.1.call-done = (f32[256,256]{1,0:T(8,128)}, f32[256,256]{1,0:T(8,128)}) async-done(((f32[256,256]{1,0:T(8,128)}, f32[256,256]{1,0:T(8,128)}), (f32[256,256]{1,0:T(8,128)}, f32[256,256]{1,0:T(8,128)})) %all-reduce.5.cloned.1.call-update) | async-done | bytes 524304 | tf_op jit(solution)/shard_map/psum | solution.py:9
  304.4 27.3 %psum.46 = f32[256]{0:T(256)S(1)} all-reduce(f32[256]{0:T(256)S(1)} %broadcast_multiply_fusion.1), channel_id=1, replica_groups=mesh['row'=8,'rep'=16] {'rep'}, use_global_device_ids=true, to_apply=%region_7.0 | all-reduce | flops 256 | bytes 2048 | tf_op jit(solution)/shard_map/psum | solution.py:9
  331.6 20.8 %psum.47 = f32[256]{0:T(256)} all-reduce(f32[256]{0:T(256)S(1)} %psum.46), channel_id=1, replica_groups=mesh['row'=8,'rep'=16] {'row'}, use_global_device_ids=true, to_apply=%region_8.0 | all-reduce | flops 256 | bytes 2048 | tf_op jit(solution)/shard_map/psum | solution.py:10
  352.4 26.9 %reduce-scatter.5.cloned.1.call-done = bf16[256,256]{1,0:T(8,128)(2,1)} async-done(((bf16[2048,256]{1,0:T(8,128)(2,1)}), bf16[256,256]{1,0:T(8,128)(2,1)}) %reduce-scatter.5.cloned.1.call-update) | async-done | bytes 131088 | tf_op jit(solution)/shard_map/reduce_scatter | solution.py:88
  379.3 1.8 fusion.1
  381.1 81.9 %all-reduce.7.cloned.1.call-done = (f32[256,256]{1,0:T(8,128)}, f32[256,256]{1,0:T(8,128)}) async-done(((f32[256,256]{1,0:T(8,128)}, f32[256,256]{1,0:T(8,128)}), (f32[256,256]{1,0:T(8,128)}, f32[256,256]{1,0:T(8,128)})) %all-reduce.7.cloned.1.call-update) | async-done | bytes 524304 | tf_op jit(solution)/shard_map/psum | solution.py:10
  463.0 1.7 copy.20
  464.7 1.7 copy.21
  (24 shorter events, 0.2 us)
Async XLA Ops:
  7.2 1.6 copy-start
  7.2 58.0 %all-gather.3.cloned.1.call-start = ((), (), s32[]{:S(2)}) async-start(), calls=%async_computation.2 | async-start | bytes 1179648 | tf_op jit(solution)/shard_map/all_gather | solution.py:49
  9.5 134.6 %reduce-scatter.3.cloned.1.call-start = ((), (), s32[]{:S(2)}) async-start(), calls=%async_computation.3 | async-start | bytes 4456448 | tf_op jit(solution)/shard_map/reduce_scatter | solution.py:51
  65.1 12.7 %copy-start.4 = (s32[256]{0:T(256)S(1)}, s32[256]{0:T(256)}, u32[]{:S(2)}) copy-start(s32[256]{0:T(256)} %param.16) | copy-start | bytes 3076
  65.1 12.8 %copy-start.2 = (bf16[256,256]{1,0:T(8,128)(2,1)S(1)}, bf16[256,256]{1,0:T(8,128)(2,1)}, u32[]{:S(2)}) copy-start(bf16[256,256]{1,0:T(8,128)(2,1)} %constant_dynamic-slice_fusion) | copy-start | bytes 393220
  65.1 12.8 %copy-start.3 = (bf16[256,256]{1,0:T(8,128)(2,1)S(1)}, bf16[256,256]{1,0:T(8,128)(2,1)}, u32[]{:S(2)}) copy-start(bf16[256,256]{1,0:T(8,128)(2,1)} %param.10) | copy-start | bytes 393220
  65.1 79.0 %copy-start.5 = (bf16[256,256]{1,0:T(8,128)(2,1)S(1)}, bf16[256,256]{1,0:T(8,128)(2,1)}, u32[]{:S(2)}) copy-start(bf16[256,256]{1,0:T(8,128)(2,1)} %param.17) | copy-start | bytes 393220
  65.1 79.0 %copy-start.6 = (bf16[256,256]{1,0:T(8,128)(2,1)S(1)}, bf16[256,256]{1,0:T(8,128)(2,1)}, u32[]{:S(2)}) copy-start(bf16[256,256]{1,0:T(8,128)(2,1)} %param.11) | copy-start | bytes 393220
  65.1 79.0 %copy-start.7 = (f32[256]{0:T(256)S(1)}, f32[256]{0:T(256)}, u32[]{:S(2)}) copy-start(f32[256]{0:T(256)} %param.12) | copy-start | bytes 3076
  77.8 106.3 %all-gather.5.cloned.1.call-start = ((), (), s32[]{:S(2)}) async-start(), calls=%async_computation.4 | async-start | bytes 2228224 | tf_op jit(solution)/shard_map/all_gather | solution.py:84
  147.0 157.3 %all-reduce.5.cloned.1.call-start = ((), (), s32[]{:S(2)}) async-start(), calls=%async_computation.6 | async-start | bytes 1048576 | tf_op jit(solution)/shard_map/psum | solution.py:9
  150.0 316.4 %copy-start.1 = (bf16[4096,256]{1,0:T(8,128)(2,1)S(1)}, bf16[4096,256]{1,0:T(8,128)(2,1)}, u32[]{:S(2)}) copy-start(bf16[4096,256]{1,0:T(8,128)(2,1)} %param.9) | copy-start | bytes 6291460
  150.0 229.3 %reduce-scatter.5.cloned.1.call-start = ((), (), s32[]{:S(2)}) async-start(), calls=%async_computation.5 | async-start | bytes 1179648 | tf_op jit(solution)/shard_map/reduce_scatter | solution.py:88
  196.4 266.6 %all-reduce.7.cloned.1.call-start = ((), (), s32[]{:S(2)}) async-start(), calls=%async_computation.7 | async-start | bytes 1048576 | tf_op jit(solution)/shard_map/psum | solution.py:10
Sparse Core Ops, SparseCore 0:
  11.0 48.4 all-gather.2
  77.9 66.1 reduce-scatter.2
  147.1 36.9 all-gather.4
  187.0 117.2 all-reduce.4
  308.2 71.0 reduce-scatter.4
  381.7 81.2 all-reduce.6
